TPU v7x, 128 devices: a whole 4x4x4 slice. The times are simulated.
128 devices in a mesh: prow: 32 (over x, z_lo, y), pcol: 4 (over z_hi, core).
Axes of the slice: x: 4, y: 4, z: 4 (z_hi: 2, z_lo: 2; z = z_hi * 2 + z_lo), core: 2. Of those that a mesh axis runs over, the one named last changes fastest.
Arguments:
- inverse_band: float32 [4096, 4096], P('prow', 'pcol'), may hold values from -0.09375 to 0.09375
- factor_panel: float32 [2, 4096, 512], P(None, 'prow', 'pcol'), may hold values from -0.6 to 0.6
- diag_inverse: float32 [2, 512, 512], replicated, may hold values from -1 to 2, as said below
- ancestors: int32 [2, 63], replicated, may hold values from 0 to 63, as said below
- counts: int32 [2], replicated, may hold values from 1 to 63, as said below
Outputs:
- new_column: float32 [2, 4096, 512], P(None, 'prow', 'pcol')
- diag_block: float32 [2, 512, 512], P(None, 'prow', 'pcol')
Inputs may be any that keep to these rules, and one draw needn't show every extreme that they name: Each row holds distinct block numbers; its first counts[s] entries are in increasing order and include 63; the entries after them are other block numbers, which are not ancestors. One of the two counts is 63; the other is below 63. `diag_inverse`: lower triangular; diagonal entries from 0.5 to 2.
All inputs are finite; a program needn't handle non-finite values.
Results may differ from a plain program's by a relative error of at most 0.000073.
Values sent between devices are 32-bit elements; how exact they have to be, the bound alone decides.
No kernel may reach another device: no remote copies, remote signals or barrier semaphores. Data moves between devices by JAX's collectives and lax.ppermute only.
A program may use at most 64 MiB of HBM per device.

v0:
```python
import jax
import jax.numpy as jnp
from jax import lax
from jax.sharding import PartitionSpec as P

W = 512
BS = 64
precise = lax.Precision.HIGHEST


def local(inverse_band, factor_panel, diag_inverse, ancestors, counts):
    row_index = lax.axis_index("prow")
    col_index = lax.axis_index("pcol")
    row_devices = lax.axis_size("prow")
    col_devices = lax.axis_size("pcol")
    supernodes = factor_panel.shape[0]
    band_rows = factor_panel.shape[1]
    blocks = band_rows // BS
    quarter = W // col_devices
    block_ids = jnp.arange(blocks, dtype=jnp.int32) * row_devices + row_index
    filled = jnp.arange(ancestors.shape[1], dtype=jnp.int32)[None, :] < counts[:, None]
    matches = (ancestors[:, :, None] == block_ids[None, None, :]) & filled[:, :, None]
    members = jnp.any(matches, axis=1).astype(jnp.float32)
    row_mask = jnp.repeat(members, BS, axis=1)[:, :, None]
    full_panel = lax.all_gather(factor_panel, "pcol", axis=2, tiled=True)
    scaled_panel = (
        jnp.einsum("srk,skw->srw", full_panel, diag_inverse, precision=precise) * row_mask
    )
    own_part = lax.dynamic_slice_in_dim(scaled_panel, col_index * quarter, quarter, 2)
    collected = lax.all_gather(own_part, "prow", axis=1, tiled=True)
    grouped = collected.reshape(
        supernodes, row_devices // col_devices, col_devices, band_rows, quarter
    )
    incoming = lax.all_to_all(grouped, "pcol", split_axis=2, concat_axis=4, tiled=True)
    stacked = incoming.reshape(incoming.shape[0], -1, incoming.shape[-1])
    partial_sums = jnp.einsum("rc,scw->srw", inverse_band, stacked, precision=precise)
    summed = lax.psum_scatter(partial_sums, "pcol", scatter_dimension=2, tiled=True)
    applied = summed * row_mask
    new_column = -applied
    diag_rows = W // row_devices
    product = jnp.einsum("src,srw->csw", scaled_panel, applied, precision=precise)
    reduced = lax.psum_scatter(
        product.reshape(lax.axis_size("prow") * diag_rows, -1),
        "prow",
        scatter_dimension=0,
        tiled=True,
    )
    reduced = reduced.reshape(diag_rows, supernodes, quarter).transpose(1, 0, 2)
    row_factor = lax.dynamic_slice_in_dim(diag_inverse, row_index * diag_rows, diag_rows, 2)
    col_factor = lax.dynamic_slice_in_dim(diag_inverse, col_index * quarter, quarter, 2)
    diag_block = jnp.einsum("skr,skw->srw", row_factor, col_factor, precision=precise) + reduced
    return (new_column, diag_block)


def solution(mesh):
    in_specs = (P("prow", "pcol"), P(None, "prow", "pcol"), P(), P(), P())
    out_specs = (P(None, "prow", "pcol"), P(None, "prow", "pcol"))
    return jax.shard_map(local, mesh=mesh, in_specs=in_specs, out_specs=out_specs, check_vma=False)
```

profile of v0, /device:TPU:0, one launch (start us, length us, event | category | flops | bytes accessed | tf_op | source)
XLA Modules:
  0.0 451.2 jit_solution(8875050085147239257)
XLA Ops:
  7.2 0.0 all-gather.2.cloned.1.call-start
  7.2 0.9 iota_compare_fusion
  8.1 0.9 and_reduce_fusion
  9.0 0.1 broadcast_in_dim.2
  9.1 0.1 mul.33
  9.1 9.9 %all_gather.6 = f32[2,128,512]{2,1,0:T(8,128)S(1)} all-gather(f32[2,128,128]{2,1,0:T(8,128)} %param.6), channel_id=1, replica_groups=mesh['prow'=32,'pcol'=4] {'pcol'}, dimensions={2}, use_global_device_ids=true | all-gather | bytes 655360 | tf_op jit(solution)/shard_map/all_gather | solution.py:25
  19.0 1.3 convolution_multiply_fusion
  20.3 0.7 constant_dynamic-slice_fusion
  21.0 0.0 reduce-scatter.3.cloned.1.call-start
  21.1 157.6 %all-gather.2.cloned.1.call-done = f32[2,4096,128]{2,1,0:T(8,128)} async-done(((f32[2,128,128]{2,1,0:T(8,128)}), f32[2,4096,128]{2,1,0:T(8,128)}) %all-gather.2.cloned.1.call-update) | async-done | bytes 4194320 | tf_op jit(solution)/shard_map/all_gather | solution.py:30
  178.7 2.5 copy.21
  181.1 53.7 %all_to_all.15 = f32[2,8,4,128,128]{4,3,1,0,2:T(8,128)} all-to-all(f32[2,8,4,128,128]{4,3,1,0,2:T(8,128)S(1)} %copy.21), channel_id=1, replica_groups=mesh['prow'=32,'pcol'=4] {'pcol'}, dimensions={2} | all-to-all | bytes 8388608 | tf_op jit(solution)/shard_map/all_to_all | solution.py:34
  234.9 5.2 %copy.22 = f32[2,8,1,128,4,128]{3,1,5,4,0,2:T(8,128)} copy(f32[2,8,1,128,4,128]{5,3,1,0,4,2:T(8,128)} %bitcast.31) | data formatting | bytes 8388608 | tf_op jit(solution)/shard_map/all_to_all | solution.py:34
  240.1 5.0 %reshape.46 = f32[2,1024,512]{1,2,0:T(8,128)} reshape(f32[2,8,1,128,4,128]{3,1,5,4,0,2:T(8,128)} %copy.22) | data formatting | bytes 8388608 | tf_op jit(solution)/shard_map/reshape | solution.py:35
  245.1 6.4 %convolution_bitcast_fusion = f32[2,128,512]{1,2,0:T(8,128)} fusion(f32[2,1024,512]{1,2,0:T(8,128)} %reshape.46, f32[128,1024]{1,0:T(8,128)S(1)} %copy-done.1), kind=kOutput, calls=%fused_computation | convolution fusion | flops 1610612736 | bytes 5242880 | tf_op jit(solution)/shard_map/rc,scw->srw/dot_general | solution.py:36
  251.5 0.0 reduce-scatter.3.cloned.1.call-update
  251.5 0.0 reduce-scatter.5.cloned.1.call-start
  251.6 27.0 %reduce-scatter.3.cloned.1.call-done = f32[2,128,128]{1,2,0:T(8,128)} async-done(((f32[2,128,512]{1,2,0:T(8,128)}), f32[2,128,128]{1,2,0:T(8,128)}) %reduce-scatter.3.cloned.1.call-update) | async-done | bytes 131088 | tf_op jit(solution)/shard_map/reduce_scatter | solution.py:37
  278.5 1.5 fusion.3
  280.0 1.0 copy.24
  281.0 0.9 multiply_negate_fusion
  282.0 0.8 copy.26
  282.7 159.5 %reduce-scatter.5.cloned.1.call-done = f32[16,256]{1,0:T(8,128)} async-done(((f32[512,256]{1,0:T(8,128)}), f32[16,256]{1,0:T(8,128)}) %reduce-scatter.5.cloned.1.call-update) | async-done | bytes 16400 | tf_op jit(solution)/shard_map/reduce_scatter | solution.py:42
  442.2 2.5 convolution_add_fusion
  (8 shorter events, 0.1 us)
Async XLA Ops:
  7.2 11.8 %copy-start = (f32[2,512,512]{2,1,0:T(8,128)S(1)}, f32[2,512,512]{2,1,0:T(8,128)}, u32[]{:S(2)}) copy-start(f32[2,512,512]{2,1,0:T(8,128)} %param.7) | copy-start | bytes 6291460
  7.2 171.5 %all-gather.2.cloned.1.call-start = ((), (), s32[]{:S(2)}) async-start(), calls=%async_computation.3 | async-start | bytes 4325376 | tf_op jit(solution)/shard_map/all_gather | solution.py:30
  21.0 257.5 %reduce-scatter.3.cloned.1.call-start = ((), (), s32[]{:S(2)}) async-start(), calls=%async_computation.4 | async-start | bytes 655360 | tf_op jit(solution)/shard_map/reduce_scatter | solution.py:37
  240.1 5.0 %copy-start.1 = (f32[128,1024]{1,0:T(8,128)S(1)}, f32[128,1024]{1,0:T(8,128)}, u32[]{:S(2)}) copy-start(f32[128,1024]{1,0:T(8,128)} %param.5) | copy-start | bytes 1572868
  251.5 190.7 %reduce-scatter.5.cloned.1.call-start = ((), (), s32[]{:S(2)}) async-start(), calls=%async_computation.5 | async-start | bytes 540672 | tf_op jit(solution)/shard_map/reduce_scatter | solution.py:42
Sparse Core Ops, SparseCore 0:
  21.1 157.5 all-gather.1
  251.6 26.8 reduce-scatter.2
  281.2 161.0 reduce-scatter.4
where the time goes:
time: 452 us; the launch traced here: 451 us
  waiting for transfers between devices  344 us (76%)
  blocking collectives  63.6 us (14%)
  local copies, waits for them, and re-layouts  15.3 us (3%)
  between operations  13.8 us (3%)
  matrix products  11.7 us (3%)
    reduce_scatter x1, waiting for transfers between devices, local(): lax.psum_scatter(product.reshape(lax.axis_size('prow') * diag_rows, -1),...  159 us
    all_gather x1, waiting for transfers between devices, local(): collected = lax.all_gather(own_part, 'prow', axis=1, tiled=True)  158 us
    all_to_all x1, blocking collectives, local(): lax.all_to_all(grouped, 'pcol', split_axis=2, concat_axis=4, tiled=True)  53.7 us
    reduce_scatter x1, waiting for transfers between devices, local(): lax.psum_scatter(partial_sums, 'pcol', scatter_dimension=2, tiled=True)  27 us
    all_gather x1, blocking collectives, local(): full_panel = lax.all_gather(factor_panel, 'pcol', axis=2, tiled=True)  9.87 us
  transfers between devices with their start and end apart: 3, of which 3 were waited for; matrix products, arithmetic and copies ran while one was open for 0% of the time, Pallas kernels for 0%

commit v1 on v0

--- a/solution.py
+++ b/solution.py
@@ -2,10 +2,23 @@
 import jax.numpy as jnp
 from jax import lax
 from jax.sharding import PartitionSpec as P
+from jax.lax import all_to_all, axis_size
 
 W = 512
 BS = 64
 precise = lax.Precision.HIGHEST
+
+
+def register_the_stocks(arr_in, group_axis, which_dim):
+    return jnp.concatenate(
+        all_to_all(
+            jnp.stack(axis_size(group_axis) * [arr_in], axis=0),
+            concat_axis=0,
+            axis_name=group_axis,
+            split_axis=0,
+        ),
+        which_dim,
+    )
 
 
 def local(inverse_band, factor_panel, diag_inverse, ancestors, counts):
@@ -27,7 +40,7 @@
         jnp.einsum("srk,skw->srw", full_panel, diag_inverse, precision=precise) * row_mask
     )
     own_part = lax.dynamic_slice_in_dim(scaled_panel, col_index * quarter, quarter, 2)
-    collected = lax.all_gather(own_part, "prow", axis=1, tiled=True)
+    collected = register_the_stocks(own_part, "prow", 1)
     grouped = collected.reshape(
         supernodes, row_devices // col_devices, col_devices, band_rows, quarter
     )

time: 452 us -> 350 us (0.77)
  waiting for transfers between devices: 344 us -> 186 us
  blocking collectives: 63.6 us -> 122 us
    all_gather x1 -> x0, waiting for transfers between devices: 158 us -> none  [local(): collected = lax.all_gather(own_part, 'prow', axis=1, tiled=True)]
    all_to_all x0 -> x1, blocking collectives: none -> 58.2 us  [register_the_stocks(): all_to_all(jnp.stack(axis_size(group_axis) * [arr_in], axis=0), concat_ax...]
  transfers between devices with their start and end apart: 3 -> 2, of which waited for: 3 -> 2; matrix products, arithmetic and copies ran while one was open for 0% -> 0% of each run, Pallas kernels for 0% -> 0%
where the time goes in v1:
time: 350 us
  waiting for transfers between devices  186 us (53%)
  blocking collectives  122 us (35%)
  between operations  14.1 us (4%)
  local copies, waits for them, and re-layouts  13.1 us (4%)
  matrix products  11.7 us (3%)
    reduce_scatter x1, waiting for transfers between devices, local(): lax.psum_scatter(product.reshape(lax.axis_size('prow') * diag_rows, -1),...  160 us
    all_to_all x1, blocking collectives, register_the_stocks(): all_to_all(jnp.stack(axis_size(group_axis) * [arr_in], axis=0), concat_ax...  58.2 us
    all_to_all x1, blocking collectives, local(): lax.all_to_all(grouped, 'pcol', split_axis=2, concat_axis=4, tiled=True)  54 us
    reduce_scatter x1, waiting for transfers between devices, local(): lax.psum_scatter(partial_sums, 'pcol', scatter_dimension=2, tiled=True)  26.1 us
    all_gather x1, blocking collectives, local(): full_panel = lax.all_gather(factor_panel, 'pcol', axis=2, tiled=True)  9.87 us
  transfers between devices with their start and end apart: 2, of which 2 were waited for; matrix products, arithmetic and copies ran while one was open for 0% of the time, Pallas kernels for 0%

profile of v1, /device:TPU:0, one launch (start us, length us, event | category | flops | bytes accessed | tf_op | source)
XLA Modules:
  0.0 349.7 jit_solution(1106226784478211457)
XLA Ops:
  7.2 0.0 reduce-scatter.3.cloned.1.call-start
  7.2 0.9 iota_compare_fusion
  8.1 0.9 and_reduce_fusion
  9.0 0.1 broadcast_in_dim.2
  9.1 0.1 mul.33
  9.1 9.9 %all_gather.3 = f32[2,128,512]{2,1,0:T(8,128)S(1)} all-gather(f32[2,128,128]{2,1,0:T(8,128)} %param.6), channel_id=1, replica_groups=mesh['prow'=32,'pcol'=4] {'pcol'}, dimensions={2}, use_global_device_ids=true | all-gather | bytes 655360 | tf_op jit(solution)/shard_map/all_gather | solution.py:38
  19.0 1.3 convolution_multiply_fusion
  20.3 0.5 stack.2
  20.8 58.2 %all_to_all.20 = f32[32,2,128,128]{3,2,1,0:T(8,128)S(1)} all-to-all(f32[32,2,128,128]{3,2,1,0:T(8,128)S(1)} %stack.2), channel_id=1, replica_groups=mesh['prow'=32,'pcol'=4] {'prow'}, dimensions={0} | all-to-all | bytes 8388608 | tf_op jit(solution)/shard_map/all_to_all | solution.py:14
  79.0 0.5 copy.22
  79.5 54.0 %all_to_all.21 = f32[2,8,4,128,128]{4,3,1,0,2:T(8,128)} all-to-all(f32[2,8,4,128,128]{4,3,1,0,2:T(8,128)S(1)} %copy.22), channel_id=1, replica_groups=mesh['prow'=32,'pcol'=4] {'pcol'}, dimensions={2} | all-to-all | bytes 8388608 | tf_op jit(solution)/shard_map/all_to_all | solution.py:47
  133.5 5.2 %copy.23 = f32[2,8,1,128,4,128]{3,1,5,4,0,2:T(8,128)} copy(f32[2,8,1,128,4,128]{5,3,1,0,4,2:T(8,128)} %bitcast.34) | data formatting | bytes 8388608 | tf_op jit(solution)/shard_map/all_to_all | solution.py:47
  138.8 5.0 %reshape.48 = f32[2,1024,512]{1,2,0:T(8,128)} reshape(f32[2,8,1,128,4,128]{3,1,5,4,0,2:T(8,128)} %copy.23) | data formatting | bytes 8388608 | tf_op jit(solution)/shard_map/reshape | solution.py:48
  143.7 6.4 %convolution_bitcast_fusion = f32[2,128,512]{1,2,0:T(8,128)} fusion(f32[2,1024,512]{1,2,0:T(8,128)} %reshape.48, f32[128,1024]{1,0:T(8,128)S(1)} %copy-done.1), kind=kOutput, calls=%fused_computation | convolution fusion | flops 1610612736 | bytes 5242880 | tf_op jit(solution)/shard_map/rc,scw->srw/dot_general | solution.py:49
  150.1 0.0 reduce-scatter.3.cloned.1.call-update
  150.2 0.0 reduce-scatter.5.cloned.1.call-start
  150.2 26.1 %reduce-scatter.3.cloned.1.call-done = f32[2,128,128]{1,2,0:T(8,128)} async-done(((f32[2,128,512]{1,2,0:T(8,128)}), f32[2,128,128]{1,2,0:T(8,128)}) %reduce-scatter.3.cloned.1.call-update) | async-done | bytes 131088 | tf_op jit(solution)/shard_map/reduce_scatter | solution.py:50
  176.3 1.5 fusion.3
  177.8 1.0 copy.25
  178.8 0.0 reduce-scatter.5.cloned.1.call-update
  178.8 0.9 multiply_negate_fusion
  179.8 0.8 copy.27
  180.5 159.9 %reduce-scatter.5.cloned.1.call-done = f32[16,256]{1,0:T(8,128)} async-done(((f32[512,256]{1,0:T(8,128)}), f32[16,256]{1,0:T(8,128)}) %reduce-scatter.5.cloned.1.call-update) | async-done | bytes 16400 | tf_op jit(solution)/shard_map/reduce_scatter | solution.py:55
  340.4 2.5 convolution_add_fusion
  (7 shorter events, 0.1 us)
Async XLA Ops:
  7.2 11.8 %copy-start = (f32[2,512,512]{2,1,0:T(8,128)S(1)}, f32[2,512,512]{2,1,0:T(8,128)}, u32[]{:S(2)}) copy-start(f32[2,512,512]{2,1,0:T(8,128)} %param.7) | copy-start | bytes 6291460
  7.2 169.1 %reduce-scatter.3.cloned.1.call-start = ((), (), s32[]{:S(2)}) async-start(), calls=%async_computation.4 | async-start | bytes 655360 | tf_op jit(solution)/shard_map/reduce_scatter | solution.py:50
  138.8 5.0 %copy-start.1 = (f32[128,1024]{1,0:T(8,128)S(1)}, f32[128,1024]{1,0:T(8,128)}, u32[]{:S(2)}) copy-start(f32[128,1024]{1,0:T(8,128)} %param.5) | copy-start | bytes 1572868
  150.2 190.2 %reduce-scatter.5.cloned.1.call-start = ((), (), s32[]{:S(2)}) async-start(), calls=%async_computation.5 | async-start | bytes 540672 | tf_op jit(solution)/shard_map/reduce_scatter | solution.py:55
Sparse Core Ops, SparseCore 0:
  150.3 26.0 reduce-scatter.2
  179.0 161.3 reduce-scatter.4
